TPU v7x, 32 devices: a whole 2x2x4 slice. The times are simulated.
32 devices in a mesh: groups: 2 (over y), ctx: 4 (over z), dp: 2 (over x), rep: 2 (over core).
Axes of the slice: x: 2, y: 2, z: 4, core: 2. Of those that a mesh axis runs over, the one named last changes fastest.
Arguments:
- features: float32 [8, 4096, 128], P(('groups', 'dp', 'rep'), 'ctx'), parts along dimension 0, may hold values from -6 to 6
- cotangent: float32 [8, 4096, 128], P(('groups', 'dp', 'rep'), 'ctx'), parts along dimension 0, may hold values from -6 to 6
- norm_gains: float32 [2, 128], replicated, may hold values from 0.5 to 1.5
- depth_taps: float32 [2, 7, 128], replicated, may hold values from -2 to 2
- w_in: float32 [2, 128, 256], replicated, may hold values from -0.5 to 0.5
- w_out: float32 [2, 256, 128], replicated, may hold values from -0.375 to 0.375
Outputs:
- grad_features: float32 [8, 4096, 128], P(('groups', 'dp', 'rep'), 'ctx'), parts along dimension 0
- grad_gains: float32 [4, 128], P('groups'), parts along dimension 0
- grad_taps: float32 [4, 7, 128], P('groups'), parts along dimension 0
- grad_w_in: float32 [4, 128, 256], P('groups'), parts along dimension 0
- grad_w_out: float32 [4, 256, 128], P('groups'), parts along dimension 0
There are 2 independent parts, one for each index of `groups`. A program takes and returns all parts, laid end to end along the dimension named above; an argument that names none is the same for every part. Nothing has to cross between parts.
All inputs are finite; a program needn't handle non-finite values.
Results may differ from a plain program's by a relative error of at most 0.0001.
Values sent between devices are 32-bit elements; how exact they have to be, the bound alone decides.
A program may use at most 64 MiB of HBM per device.

v0:
```python
import jax
import jax.numpy as jnp
from jax import lax
from jax.sharding import PartitionSpec as P

FIRST_SPACING = 16
SECOND_SPACING = 256
BLOCKS = 2


STABILIZER = 1e-06


def with_halo(block, sides, width):
    for axis, dim in sides:
        count = lax.axis_size(axis)
        forward = [(i, i + 1) for i in range(count - 1)]
        backward = [(target, source) for source, target in forward]
        low = lax.ppermute(
            lax.slice_in_dim(block, block.shape[dim] - width, None, axis=dim), axis, forward
        )
        high = lax.ppermute(lax.slice_in_dim(block, 0, width, axis=dim), axis, backward)
        block = jnp.concatenate([low, block, high], axis=dim)
    return block


def rms_norm(stream, gain_vec):
    scale = lax.rsqrt(jnp.mean(stream * stream, axis=-1, keepdims=True) + STABILIZER)
    return stream * scale * gain_vec


def depth_sweep(padded, tap_weights, dilation, row_count):
    total = tap_weights[0] * padded[:, 0:row_count]
    for offset in range(1, tap_weights.shape[0]):
        total = (
            total
            + tap_weights[offset] * padded[:, offset * dilation : offset * dilation + row_count]
        )
    return total


def forward_block(stream, gain_vec, tap_weights, w_in, w_out, dilation):
    rim_width = tap_weights.shape[0] // 2 * dilation
    normed = rms_norm(stream, gain_vec)
    padded = with_halo(normed, (("ctx", 1),), rim_width)
    conv_out = depth_sweep(padded, tap_weights, dilation, stream.shape[1])
    pre_act = jnp.einsum("brc,ch->brh", conv_out, w_in, precision=lax.Precision.HIGHEST)
    act_out = jax.nn.silu(pre_act)
    result = stream + jnp.einsum("brh,hc->brc", act_out, w_out, precision=lax.Precision.HIGHEST)
    return (result, (stream, padded, conv_out, pre_act, act_out))


def backward_block(grad_out, saved_state, gain_vec, tap_weights, w_in, w_out, dilation):
    stream, padded, conv_out, pre_act, act_out = saved_state
    row_count = stream.shape[1]
    tap_count = tap_weights.shape[0]
    rim_width = tap_count // 2 * dilation
    grad_wout = jnp.einsum("brh,brc->hc", act_out, grad_out, precision=lax.Precision.HIGHEST)
    activation_gradient = jnp.einsum(
        "brc,hc->brh", grad_out, w_out, precision=lax.Precision.HIGHEST
    )
    sigmoid_val = jax.nn.sigmoid(pre_act)
    grad_pre = activation_gradient * (sigmoid_val * (1.0 + pre_act * (1.0 - sigmoid_val)))
    grad_win = jnp.einsum("brc,brh->ch", conv_out, grad_pre, precision=lax.Precision.HIGHEST)
    grad_conv = jnp.einsum("brh,ch->brc", grad_pre, w_in, precision=lax.Precision.HIGHEST)
    grad_tapw = jnp.stack(
        [
            jnp.sum(
                grad_conv * padded[:, offset * dilation : offset * dilation + row_count],
                axis=(0, 1),
            )
            for offset in range(tap_count)
        ]
    )
    grad_rims = with_halo(grad_conv, (("ctx", 1),), rim_width)
    grad_norm = depth_sweep(grad_rims, tap_weights[::-1], dilation, row_count)
    unused_out, norm_back = jax.vjp(rms_norm, stream, gain_vec)
    grad_stream, grad_gain = norm_back(grad_norm)
    return (grad_stream + grad_out, (grad_gain, grad_tapw, grad_win, grad_wout))


def local(features, cotangent, norm_gains, depth_taps, w_in, w_out):
    spacing_list = (FIRST_SPACING, SECOND_SPACING)
    stream = features
    saved_list = []
    for block_index in range(BLOCKS):
        stream, saved_state = forward_block(
            stream,
            norm_gains[block_index],
            depth_taps[block_index],
            w_in[block_index],
            w_out[block_index],
            spacing_list[block_index],
        )
        saved_list.append(saved_state)
    grad_flow = cotangent
    block_grads = [None] * BLOCKS
    for block_index in reversed(range(BLOCKS)):
        grad_flow, local_grads = backward_block(
            grad_flow,
            saved_list[block_index],
            norm_gains[block_index],
            depth_taps[block_index],
            w_in[block_index],
            w_out[block_index],
            spacing_list[block_index],
        )
        block_grads[block_index] = local_grads
    gain_total = jnp.stack([block_grads[index_b][0] for index_b in range(BLOCKS)])
    taps_total = jnp.stack([block_grads[index_b][1] for index_b in range(BLOCKS)])
    input_weight_sum = jnp.stack([block_grads[index_b][2] for index_b in range(BLOCKS)])
    wout_total = jnp.stack([block_grads[index_b][3] for index_b in range(BLOCKS)])
    gain_total, taps_total, input_weight_sum, wout_total = lax.psum(
        (gain_total, taps_total, input_weight_sum, wout_total), ("ctx", "dp", "rep")
    )
    return (grad_flow, gain_total, taps_total, input_weight_sum, wout_total)


def solution(mesh):
    return jax.shard_map(
        local,
        mesh=mesh,
        in_specs=(
            P(("groups", "dp", "rep"), "ctx", None),
            P(("groups", "dp", "rep"), "ctx", None),
            P(),
            P(),
            P(),
            P(),
        ),
        out_specs=(
            P(("groups", "dp", "rep"), "ctx", None),
            P("groups", None),
            P("groups", None, None),
            P("groups", None, None),
            P("groups", None, None),
        ),
        check_vma=False,
    )
```

profile of v0, /device:TPU:0, one launch (start us, length us, event | category | flops | bytes accessed | tf_op | source)
XLA Modules:
  0.0 170.9 jit_solution(2257633979996218653)
XLA Ops:
  8.0 1.2 multiply_reduce_fusion.19
  9.5 1.3 collective-permute-start.1
  10.8 5.6 %collective-permute-start = (f32[1,48,128]{2,1,0:T(8,128)S(1)}, f32[1,48,128]{2,1,0:T(8,128)S(1)}, u32[]{:S(2)}, u32[]{:S(2)}) collective-permute-start(f32[1,48,128]{2,1,0:T(8,128)S(1)} %get-tuple-element.47), channel_id=1, source_target_pairs={{0,4},{4,8},{8,12},{1,5},{5,9},{9,13},{2,6},{6,10},{10,14},{3,7},{... | collective-permute-start | bytes 73736 | tf_op jit(solution)/shard_map/ppermute | solution.py:19
  16.6 1.3 collective-permute-done
  18.9 1.0 fusion.51
  19.9 1.2 multiply_reduce_fusion.18
  21.4 1.3 collective-permute-start.3
  22.7 4.9 %collective-permute-start.2 = (f32[1,768,128]{2,1,0:T(8,128)S(1)}, f32[1,768,128]{2,1,0:T(8,128)S(1)}, u32[]{:S(2)}, u32[]{:S(2)}) collective-permute-start(f32[1,768,128]{2,1,0:T(8,128)S(1)} %get-tuple-element.45), channel_id=1, source_target_pairs={{0,4},{4,8},{8,12},{1,5},{5,9},{9,13},{2,6},{6,10},{10,14},{3,7},{... | collective-permute-start | bytes 1179656 | tf_op jit(solution)/shard_map/ppermute | solution.py:19
  27.5 6.0 %collective-permute-done.3 = f32[1,768,128]{2,1,0:T(8,128)S(1)} collective-permute-done((f32[1,768,128]{2,1,0:T(8,128)S(1)}, f32[1,768,128]{2,1,0:T(8,128)S(1)}, u32[]{:S(2)}, u32[]{:S(2)}) %collective-permute-start.3) | collective-permute-done | bytes 393248 | tf_op jit(solution)/shard_map/ppermute | solution.py:22
  33.5 1.2 collective-permute-done.2
  35.0 1.0 fusion.48
  36.0 1.0 copy-done.3
  37.0 1.1 convolution_multiply_fusion.1
  38.1 1.7 multiply_reduce_fusion
  40.8 4.4 %collective-permute-start.4 = (f32[1,768,128]{2,1,0:T(8,128)}, f32[1,768,128]{2,1,0:T(8,128)S(1)}, u32[]{:S(2)}, u32[]{:S(2)}) collective-permute-start(f32[1,768,128]{2,1,0:T(8,128)} %get-tuple-element.42), channel_id=1, source_target_pairs={{0,4},{4,8},{8,12},{1,5},{5,9},{9,13},{2,6},{6,10},{10,14},{3,7},{... | collective-permute-start | bytes 1179656 | tf_op jit(solution)/shard_map/ppermute | solution.py:19
  45.2 1.5 collective-permute-start.5
  46.6 1.3 stack.103
  47.9 2.4 %convolution_bitcast_fusion.3 = f32[1,128,256]{2,1,0:T(8,128)S(1)} fusion(f32[1024,256]{1,0:T(8,128)} %copy-done.5, f32[1,1024,128]{2,1,0:T(8,128)S(1)} %multiply_add_fusion), kind=kOutput, calls=%fused_computation.6 | convolution fusion | flops 402653184 | bytes 1703936 | tf_op jit(solution)/shard_map/brc,brh->ch/dot_general | solution.py:64
  50.4 1.9 %convolution_bitcast_fusion.1 = f32[1,256,128]{2,1,0:T(8,128)S(1)} fusion(f32[1024,256]{1,0:T(8,128)S(1)} %copy-done.4, f32[1,1024,128]{2,1,0:T(8,128)S(1)} %copy-done.7), kind=kOutput, calls=%fused_computation.4 | convolution fusion | flops 403701760 | bytes 1703936 | tf_op jit(solution)/shard_map/brh,brc->hc/dot_general | solution.py:58
  52.3 3.5 %collective-permute-done.5 = f32[1,768,128]{2,1,0:T(8,128)} collective-permute-done((f32[1,768,128]{2,1,0:T(8,128)}, f32[1,768,128]{2,1,0:T(8,128)}, u32[]{:S(2)}, u32[]{:S(2)}) %collective-permute-start.5) | collective-permute-done | bytes 393248 | tf_op jit(solution)/shard_map/ppermute | solution.py:22
  55.9 1.7 multiply_reduce_fusion.14
  58.8 1.9 %convolution_bitcast_fusion.2 = f32[1,256,128]{2,1,0:T(8,128)S(1)} fusion(f32[1,1024,128]{2,1,0:T(8,128)S(1)} %fusion.21, f32[1024,256]{1,0:T(8,128)S(1)} %copy-done.2), kind=kOutput, calls=%fused_computation.5 | convolution fusion | flops 403701760 | bytes 1703936 | tf_op jit(solution)/shard_map/brh,brc->hc/dot_general | solution.py:58
  60.7 1.1 convolution_multiply_fusion
  61.9 1.0 convolution_bitcast_fusion.4
  63.0 1.0 multiply_reduce_fusion.7
  64.0 3.3 %collective-permute-start.6 = (f32[1,48,128]{2,1,0:T(8,128)S(1)}, f32[1,48,128]{2,1,0:T(8,128)S(1)}, u32[]{:S(2)}, u32[]{:S(2)}) collective-permute-start(f32[1,48,128]{2,1,0:T(8,128)S(1)} %get-tuple-element.40), channel_id=1, source_target_pairs={{0,4},{4,8},{8,12},{1,5},{5,9},{9,13},{2,6},{6,10},{10,14},{3,7},{... | collective-permute-start | bytes 73736 | tf_op jit(solution)/shard_map/ppermute | solution.py:19
  67.4 1.3 collective-permute-start.7
  70.9 2.2 %collective-permute-done.7 = f32[1,48,128]{2,1,0:T(8,128)S(1)} collective-permute-done((f32[1,48,128]{2,1,0:T(8,128)S(1)}, f32[1,48,128]{2,1,0:T(8,128)S(1)}, u32[]{:S(2)}, u32[]{:S(2)}) %collective-permute-start.7) | collective-permute-done | bytes 24608 | tf_op jit(solution)/shard_map/ppermute | solution.py:22
  73.7 31.2 %all-reduce = (f32[2,128]{1,0:T(2,128)}, f32[2,7,128]{2,1,0:T(8,128)S(1)}) all-reduce(f32[2,128]{1,0:T(2,128)S(1)} %pad_maximum_fusion.11, f32[2,7,128]{2,1,0:T(8,128)S(1)} %pad_maximum_fusion.10), channel_id=1, replica_groups=mesh['groups'=2,'ctx'=4,'dp'=2,'rep'=2] {'ctx','dp','rep'}, use_global_device_ids=true, to_apply=%region_6.7 | all-reduce | flops 2048 | bytes 16384 | tf_op jit(solution)/shard_map/psum | solution.py:113
  105.5 1.1 fusion.22
  106.6 55.0 %all-reduce.4.cloned.1.call-done = (f32[2,128,256]{2,1,0:T(8,128)}, f32[2,256,128]{2,1,0:T(8,128)}) async-done(((f32[2,128,256]{2,1,0:T(8,128)}, f32[2,256,128]{2,1,0:T(8,128)}), (f32[2,128,256]{2,1,0:T(8,128)}, f32[2,256,128]{2,1,0:T(8,128)})) %all-reduce.4.cloned.1.call-update) | async-done | bytes 524304 | tf_op jit(solution)/shard_map/psum | solution.py:113
  161.7 1.7 %copy.14 = f32[2,128,256]{2,1,0:T(8,128)} copy(f32[2,128,256]{2,1,0:T(8,128)} %get-tuple-element.71) | data formatting | bytes 524288
  (129 shorter events, 8.8 us)
Async XLA Ops:
  7.2 154.5 %all-reduce.4.cloned.1.call-start = ((), (), s32[]{:S(2)}) async-start(), calls=%async_computation | async-start | bytes 1048576 | tf_op jit(solution)/shard_map/psum | solution.py:113
  8.0 13.1 %copy-start.18 = (f32[128]{0:T(128)}, f32[128]{0:T(128)S(1)}, u32[]{:S(2)}) copy-start(f32[128]{0:T(128)S(1)} %get-tuple-element.62) | copy-start | bytes 1540
  9.5 6.9 %copy-start.20 = (f32[2,7,128]{2,0,1:T(2,128)S(1)}, f32[2,7,128]{2,0,1:T(2,128)}, u32[]{:S(2)}) copy-start(f32[2,7,128]{2,0,1:T(2,128)} %param.9) | copy-start | bytes 21508
  9.5 7.0 %collective-permute-start.1 = (f32[1,48,128]{2,1,0:T(8,128)S(1)}, f32[1,48,128]{2,1,0:T(8,128)S(1)}, u32[]{:S(2)}, u32[]{:S(2)}) collective-permute-start(f32[1,48,128]{2,1,0:T(8,128)S(1)} %get-tuple-element.46), channel_id=1, source_target_pairs={{4,0},{8,4},{12,8},{5,1},{9,5},{13,9},{6,2},{10,6},{14,10},{7,3},{... | collective-permute-start | bytes 73736 | tf_op jit(solution)/shard_map/ppermute | solution.py:22
  10.8 7.1 %collective-permute-start = (f32[1,48,128]{2,1,0:T(8,128)S(1)}, f32[1,48,128]{2,1,0:T(8,128)S(1)}, u32[]{:S(2)}, u32[]{:S(2)}) collective-permute-start(f32[1,48,128]{2,1,0:T(8,128)S(1)} %get-tuple-element.47), channel_id=1, source_target_pairs={{0,4},{4,8},{8,12},{1,5},{5,9},{9,13},{2,6},{6,10},{10,14},{3,7},{... | collective-permute-start | bytes 73736 | tf_op jit(solution)/shard_map/ppermute | solution.py:19
  16.5 18.2 %copy-start.35 = (f32[128]{0:T(128)}, f32[128]{0:T(128)S(1)}, u32[]{:S(2)}) copy-start(f32[128]{0:T(128)S(1)} %get-tuple-element.48) | copy-start | bytes 1540
  16.5 18.2 %copy-start.37 = (f32[128]{0:T(128)}, f32[128]{0:T(128)S(1)}, u32[]{:S(2)}) copy-start(f32[128]{0:T(128)S(1)} %get-tuple-element.49) | copy-start | bytes 1540
  16.5 18.2 %copy-start.39 = (f32[128]{0:T(128)}, f32[128]{0:T(128)S(1)}, u32[]{:S(2)}) copy-start(f32[128]{0:T(128)S(1)} %get-tuple-element.50) | copy-start | bytes 1540
  16.5 18.2 %copy-start.41 = (f32[128]{0:T(128)}, f32[128]{0:T(128)S(1)}, u32[]{:S(2)}) copy-start(f32[128]{0:T(128)S(1)} %get-tuple-element.51) | copy-start | bytes 1540
  16.5 18.2 %copy-start.43 = (f32[128]{0:T(128)}, f32[128]{0:T(128)S(1)}, u32[]{:S(2)}) copy-start(f32[128]{0:T(128)S(1)} %get-tuple-element.58) | copy-start | bytes 1540
  16.5 18.2 %copy-start.45 = (f32[128]{0:T(128)}, f32[128]{0:T(128)S(1)}, u32[]{:S(2)}) copy-start(f32[128]{0:T(128)S(1)} %get-tuple-element.60) | copy-start | bytes 1540
  16.5 18.2 %copy-start.47 = (f32[128]{0:T(128)}, f32[128]{0:T(128)S(1)}, u32[]{:S(2)}) copy-start(f32[128]{0:T(128)S(1)} %get-tuple-element.61) | copy-start | bytes 1540
  21.4 12.2 %collective-permute-start.3 = (f32[1,768,128]{2,1,0:T(8,128)S(1)}, f32[1,768,128]{2,1,0:T(8,128)S(1)}, u32[]{:S(2)}, u32[]{:S(2)}) collective-permute-start(f32[1,768,128]{2,1,0:T(8,128)S(1)} %get-tuple-element.44), channel_id=1, source_target_pairs={{4,0},{8,4},{12,8},{5,1},{9,5},{13,9},{6,2},{10,6},{14,10},{7,3},{... | collective-permute-start | bytes 1179656 | tf_op jit(solution)/shard_map/ppermute | solution.py:22
  22.7 12.0 %collective-permute-start.2 = (f32[1,768,128]{2,1,0:T(8,128)S(1)}, f32[1,768,128]{2,1,0:T(8,128)S(1)}, u32[]{:S(2)}, u32[]{:S(2)}) collective-permute-start(f32[1,768,128]{2,1,0:T(8,128)S(1)} %get-tuple-element.45), channel_id=1, source_target_pairs={{0,4},{4,8},{8,12},{1,5},{5,9},{9,13},{2,6},{6,10},{10,14},{3,7},{... | collective-permute-start | bytes 1179656 | tf_op jit(solution)/shard_map/ppermute | solution.py:19
  40.8 11.6 %collective-permute-start.4 = (f32[1,768,128]{2,1,0:T(8,128)}, f32[1,768,128]{2,1,0:T(8,128)S(1)}, u32[]{:S(2)}, u32[]{:S(2)}) collective-permute-start(f32[1,768,128]{2,1,0:T(8,128)} %get-tuple-element.42), channel_id=1, source_target_pairs={{0,4},{4,8},{8,12},{1,5},{5,9},{9,13},{2,6},{6,10},{10,14},{3,7},{... | collective-permute-start | bytes 1179656 | tf_op jit(solution)/shard_map/ppermute | solution.py:19
  45.2 10.7 %collective-permute-start.5 = (f32[1,768,128]{2,1,0:T(8,128)}, f32[1,768,128]{2,1,0:T(8,128)}, u32[]{:S(2)}, u32[]{:S(2)}) collective-permute-start(f32[1,768,128]{2,1,0:T(8,128)} %get-tuple-element.43), channel_id=1, source_target_pairs={{4,0},{8,4},{12,8},{5,1},{9,5},{13,9},{6,2},{10,6},{14,10},{7,3},{... | collective-permute-start | bytes 1179656 | tf_op jit(solution)/shard_map/ppermute | solution.py:22
  47.9 2.4 %copy-start.4 = (f32[1024,256]{1,0:T(8,128)S(1)}, f32[1024,256]{1,0:T(8,128)}, u32[]{:S(2)}) copy-start(f32[1024,256]{1,0:T(8,128)} %copy-done.3) | copy-start | bytes 3145732
  47.9 2.4 %copy-start.7 = (f32[1,1024,128]{2,1,0:T(8,128)S(1)}, f32[1,1024,128]{2,1,0:T(8,128)}, u32[]{:S(2)}) copy-start(f32[1,1024,128]{2,1,0:T(8,128)} %param.7) | copy-start | bytes 1572868
  50.3 5.5 %copy-start.19 = (f32[128]{0:T(128)S(1)}, f32[128]{0:T(128)}, u32[]{:S(2)}) copy-start(f32[128]{0:T(128)} %copy-done.18) | copy-start | bytes 1540
  50.4 5.5 %copy-start.36 = (f32[128]{0:T(128)S(1)}, f32[128]{0:T(128)}, u32[]{:S(2)}) copy-start(f32[128]{0:T(128)} %copy-done.35) | copy-start | bytes 1540
  50.4 5.5 %copy-start.38 = (f32[128]{0:T(128)S(1)}, f32[128]{0:T(128)}, u32[]{:S(2)}) copy-start(f32[128]{0:T(128)} %copy-done.37) | copy-start | bytes 1540
  50.4 5.5 %copy-start.40 = (f32[128]{0:T(128)S(1)}, f32[128]{0:T(128)}, u32[]{:S(2)}) copy-start(f32[128]{0:T(128)} %copy-done.39) | copy-start | bytes 1540
  50.4 5.5 %copy-start.42 = (f32[128]{0:T(128)S(1)}, f32[128]{0:T(128)}, u32[]{:S(2)}) copy-start(f32[128]{0:T(128)} %copy-done.41) | copy-start | bytes 1540
  50.4 5.5 %copy-start.44 = (f32[128]{0:T(128)S(1)}, f32[128]{0:T(128)}, u32[]{:S(2)}) copy-start(f32[128]{0:T(128)} %copy-done.43) | copy-start | bytes 1540
  50.4 5.5 %copy-start.46 = (f32[128]{0:T(128)S(1)}, f32[128]{0:T(128)}, u32[]{:S(2)}) copy-start(f32[128]{0:T(128)} %copy-done.45) | copy-start | bytes 1540
  50.4 5.5 %copy-start.48 = (f32[128]{0:T(128)S(1)}, f32[128]{0:T(128)}, u32[]{:S(2)}) copy-start(f32[128]{0:T(128)} %copy-done.47) | copy-start | bytes 1540
  64.0 6.9 %collective-permute-start.6 = (f32[1,48,128]{2,1,0:T(8,128)S(1)}, f32[1,48,128]{2,1,0:T(8,128)S(1)}, u32[]{:S(2)}, u32[]{:S(2)}) collective-permute-start(f32[1,48,128]{2,1,0:T(8,128)S(1)} %get-tuple-element.40), channel_id=1, source_target_pairs={{0,4},{4,8},{8,12},{1,5},{5,9},{9,13},{2,6},{6,10},{10,14},{3,7},{... | collective-permute-start | bytes 73736 | tf_op jit(solution)/shard_map/ppermute | solution.py:19
  67.4 5.7 %collective-permute-start.7 = (f32[1,48,128]{2,1,0:T(8,128)S(1)}, f32[1,48,128]{2,1,0:T(8,128)S(1)}, u32[]{:S(2)}, u32[]{:S(2)}) collective-permute-start(f32[1,48,128]{2,1,0:T(8,128)S(1)} %get-tuple-element.41), channel_id=1, source_target_pairs={{4,0},{8,4},{12,8},{5,1},{9,5},{13,9},{6,2},{10,6},{14,10},{7,3},{... | collective-permute-start | bytes 73736 | tf_op jit(solution)/shard_map/ppermute | solution.py:22
  70.9 2.3 %copy-start.28 = (f32[128]{0:T(128)S(1)}, f32[128]{0:T(128)}, u32[]{:S(2)}) copy-start(f32[128]{0:T(128)} %copy-done.27) | copy-start | bytes 1540
  70.9 2.3 %copy-start.30 = (f32[128]{0:T(128)S(1)}, f32[128]{0:T(128)}, u32[]{:S(2)}) copy-start(f32[128]{0:T(128)} %copy-done.29) | copy-start | bytes 1540
  70.9 2.3 %copy-start.32 = (f32[128]{0:T(128)S(1)}, f32[128]{0:T(128)}, u32[]{:S(2)}) copy-start(f32[128]{0:T(128)} %copy-done.31) | copy-start | bytes 1540
  70.9 2.3 %copy-start.34 = (f32[128]{0:T(128)S(1)}, f32[128]{0:T(128)}, u32[]{:S(2)}) copy-start(f32[128]{0:T(128)} %copy-done.33) | copy-start | bytes 1540
  (28 other events, 41.6 us)
Sparse Core Ops, SparseCore 0:
  70.3 91.3 all-reduce.3
where the time goes:
time: 172 us; the launch traced here: 171 us
  waiting for transfers between devices  69.3 us (40%)
  blocking collectives  31.2 us (18%)
  starting transfers between devices  23.6 us (14%)
  matrix products  15.3 us (9%)
  between operations  14.9 us (9%)
  local copies, waits for them, and re-layouts  9.53 us (6%)
  other arithmetic  7.23 us (4%)
    psum x1, waiting for transfers between devices, local(): lax.psum((gain_total, taps_total, input_weight_sum, wout_total), ('ctx',...  55 us
    psum x1, blocking collectives, local(): lax.psum((gain_total, taps_total, input_weight_sum, wout_total), ('ctx',...  31.2 us
    ppermute x4, starting transfers between devices, with_halo(): lax.ppermute(lax.slice_in_dim(block, block.shape[dim] - width, None, axis...  18.2 us
    ppermute x4, waiting for transfers between devices, with_halo(): lax.ppermute(lax.slice_in_dim(block, 0, width, axis=dim), axis, backward)  11.7 us
    unnamed x105, local copies, waits for them, and re-layouts  6.46 us
    ppermute x4, starting transfers between devices, with_halo(): lax.ppermute(lax.slice_in_dim(block, 0, width, axis=dim), axis, backward)  5.35 us
    dot_general x2, matrix products, backward_block(): jnp.einsum('brh,brc->hc', act_out, grad_out, precision=lax.Precision.HIGH...  3.78 us
  transfers between devices with their start and end apart: 9, of which 6 were waited for; matrix products, arithmetic and copies ran while one was open for 5% of the time, Pallas kernels for 0%

commit v1 on v0

v1 whole, which is shorter than its diff:
```python
import functools

import jax
import jax.numpy as jnp
from jax import lax
from jax.experimental import pallas as pl
from jax.experimental.pallas import tpu as pltpu
from jax.sharding import PartitionSpec as P

D1 = 16
D2 = 256
TAPS = 7
HALF = TAPS // 2
CHUNKS = 4
RES = D2 // CHUNKS
EPS = 1e-06
F32 = jnp.float32
BF16 = jnp.bfloat16
MESH = pl.DeviceIdType.MESH
ORDER = (1, 2, 0, 3)

NN = (((1,), (0,)), ((), ()))
NT = (((1,), (1,)), ((), ()))
TN = (((0,), (0,)), ((), ()))


def split(v):
    high = v.astype(BF16)
    return high, (v - high.astype(F32)).astype(BF16)


def dot3(ah, al, bh, bl, dims):
    def dot(a, b):
        return lax.dot_general(a, b, dims, preferred_element_type=F32)

    return dot(ah, bh) + (dot(ah, bl) + dot(al, bh))


def inv_rms(v):
    return lax.rsqrt(jnp.mean(v * v, axis=-1, keepdims=True) + EPS)


def silu_pair(pre):
    s = 1.0 / (1.0 + jnp.exp(-pre))
    act = pre * s
    return act, s + act * (1.0 - s)


def kernel(
    nctx, ndp, nrep, rows_total, grad_rows,
    x_ref, ct_ref, gain_ref, taps_ref, win_ref, wout_ref,
    gx_ref, gg_ref, gt_ref, gwi_ref, gwo_ref,
    pad1, gpad1, pad2, gpad2, st1, g1,
    wih, wil, woh, wol,
    ch, cl, ah, al, dact, gh, gl, ph, plo,
    gbuf, obuf, rec_a, rec_b, rec_c, small, sm_a, sm_b, sm_c,
    send_sem, recv_sem,
):
    segs = rows_total // D2
    crow = segs * RES
    rim = HALF * D1
    zi = lax.axis_index("ctx")
    di = lax.axis_index("dp")
    ri = lax.axis_index("rep")
    has_left = zi > 0
    has_right = zi < nctx - 1
    left = lax.rem(zi + nctx - 1, nctx)
    right = lax.rem(zi + 1, nctx)
    count = [0]
    pending = []

    def remote(src, dst, device):
        i = count[0]
        count[0] += 1
        return pltpu.make_async_remote_copy(
            src_ref=src, dst_ref=dst, send_sem=send_sem.at[i], recv_sem=recv_sem.at[i],
            device_id=device, device_id_type=MESH,
        )

    barrier = pltpu.get_barrier_semaphore()
    greeted = 0
    for axis, me, n in (("ctx", zi, nctx), ("dp", di, ndp), ("rep", ri, nrep)):
        for o in range(1, n):
            pl.semaphore_signal(
                barrier, inc=1, device_id={axis: lax.rem(me + o, n)}, device_id_type=MESH
            )
            greeted += 1

    gain1 = gain_ref[0:1, :]
    gain2 = gain_ref[1:2, :]

    def norm_rows(lo, n):
        v = x_ref[0, lo:lo + n, :]
        pad1[rim + lo:rim + lo + n, :] = v * inv_rms(v) * gain1

    norm_rows(0, rim)
    norm_rows(rows_total - rim, rim)
    pl.semaphore_wait(barrier, greeted)

    class Halo:
        def __init__(self, to_right_src, to_right_dst, to_left_src, to_left_dst):
            self.r = remote(to_right_src, to_right_dst, {"ctx": right})
            self.l = remote(to_left_src, to_left_dst, {"ctx": left})

        def start(self):
            @pl.when(has_right)
            def _():
                self.r.start()

            @pl.when(has_left)
            def _():
                self.l.start()

            pending.append(self)

        def wait(self):
            @pl.when(has_left)
            def _():
                self.r.wait_recv()

            @pl.when(has_right)
            def _():
                self.l.wait_recv()

        def finish(self):
            @pl.when(has_right)
            def _():
                self.r.wait_send()

            @pl.when(has_left)
            def _():
                self.l.wait_send()

    def rim_halo(ref):
        return Halo(
            ref.at[pl.ds(rows_total, rim)], ref.at[pl.ds(0, rim)],
            ref.at[pl.ds(rim, rim)], ref.at[pl.ds(rim + rows_total, rim)],
        )

    def seg_halo(ref, c):
        return Halo(
            ref.at[c, pl.ds(segs, HALF)], ref.at[c, pl.ds(0, HALF)],
            ref.at[c, pl.ds(HALF, HALF)], ref.at[c, pl.ds(HALF + segs, HALF)],
        )

    halo1 = rim_halo(pad1)
    halo1.start()

    @pl.when(zi == 0)
    def _():
        pad1[0:rim, :] = jnp.zeros((rim, 128), F32)
        gpad1[0:rim, :] = jnp.zeros((rim, 128), F32)
        pad2[:, 0:HALF] = jnp.zeros((CHUNKS, HALF, RES, 128), F32)
        gpad2[:, 0:HALF] = jnp.zeros((CHUNKS, HALF, RES, 128), F32)

    @pl.when(zi == nctx - 1)
    def _():
        pad1[rim + rows_total:, :] = jnp.zeros((rim, 128), F32)
        gpad1[rim + rows_total:, :] = jnp.zeros((rim, 128), F32)
        pad2[:, HALF + segs:] = jnp.zeros((CHUNKS, HALF, RES, 128), F32)
        gpad2[:, HALF + segs:] = jnp.zeros((CHUNKS, HALF, RES, 128), F32)

    norm_rows(rim, rows_total - 2 * rim)
    for b in range(2):
        wih[b], wil[b] = split(win_ref[b])
        woh[b], wol[b] = split(wout_ref[b])

    def gather(ref, c, base):
        return jnp.concatenate(
            [ref[base + j * D2 + c * RES:base + j * D2 + (c + 1) * RES, :] for j in range(segs)],
            axis=0,
        )

    def tap(b, k):
        return taps_ref[b, k:k + 1, :]

    def forward_tail(b, c, conv):
        at = pl.ds(c * crow, crow)
        cth, ctl = split(conv)
        ch[b, at], cl[b, at] = cth, ctl
        pre = dot3(cth, ctl, wih[b], wil[b], NN)
        act, slope = silu_pair(pre)
        dact[b, at] = slope
        ath, atl = split(act)
        ah[b, at], al[b, at] = ath, atl

    def backward_head(b, c, g):
        at = pl.ds(c * crow, crow)
        gth, gtl = split(g)
        gh[b, at], gl[b, at] = gth, gtl
        gpre = dot3(gth, gtl, woh[b], wol[b], NT) * dact[b, at]
        pth, ptl = split(gpre)
        ph[b, at], plo[b, at] = pth, ptl
        return dot3(pth, ptl, wih[b], wil[b], NT)

    def weight_grads(b):
        gwi = dot3(ch[b], cl[b], ph[b], plo[b], TN)
        gbuf[b, 0:128, :] = gwi[:, 0:128]
        gbuf[b, 128:256, :] = gwi[:, 128:256]
        gbuf[b, 256:512, :] = dot3(ah[b], al[b], gh[b], gl[b], TN)

    halo2 = [seg_halo(pad2, c) for c in range(CHUNKS)]
    waited = False
    for c in ORDER:
        if c in (0, CHUNKS - 1) and not waited:
            halo1.wait()
            waited = True
        conv = tap(0, 0) * gather(pad1, c, 0)
        for k in range(1, TAPS):
            conv = conv + tap(0, k) * gather(pad1, c, k * D1)
        forward_tail(0, c, conv)
        at = pl.ds(c * crow, crow)
        s = gather(x_ref.at[0], c, 0) + dot3(ah[0, at], al[0, at], woh[0], wol[0], NN)
        st1[at] = s
        pad2[c, HALF:HALF + segs] = (s * inv_rms(s) * gain2).reshape(segs, RES, 128)
        halo2[c].start()

    ghalo2 = [seg_halo(gpad2, c) for c in range(CHUNKS)]
    for c in ORDER:
        halo2[c].wait()
        conv = tap(1, 0) * pad2[c, 0:segs].reshape(crow, 128)
        for k in range(1, TAPS):
            conv = conv + tap(1, k) * pad2[c, k:k + segs].reshape(crow, 128)
        forward_tail(1, c, conv)
        gconv = backward_head(1, c, gather(ct_ref.at[0], c, 0))
        gpad2[c, HALF:HALF + segs] = gconv.reshape(segs, RES, 128)
        ghalo2[c].start()

    half = grad_rows // nrep
    quarter = half // ndp
    piece = quarter // nctx
    axes = (
        ("rep", ri, nrep, rec_a, sm_a, half, 0),
        ("dp", di, ndp, rec_b, sm_b, quarter, ri * half),
        ("ctx", zi, nctx, rec_c, sm_c, piece, ri * half + di * quarter),
    )

    def rows_at(start, size):
        return pl.ds(pl.multiple_of(start, 8), size)

    def scatter_start(b, level):
        axis, me, n, rec, _, size, base = axes[level]
        copies = []
        for o in range(1, n):
            peer = lax.rem(me + o, n)
            copy = remote(
                gbuf.at[b, rows_at(base + peer * size, size)], rec.at[b, o - 1], {axis: peer}
            )
            copy.start()
            copies.append(copy)
        pending.append(copies)
        return copies

    def scatter_end(b, level, copies):
        axis, me, n, rec, _, size, base = axes[level]
        own = rows_at(base + me * size, size)
        total = gbuf[b, own, :]
        for o in range(1, n):
            copies[o - 1].wait_recv()
            total = total + rec[b, o - 1]
        if level == 2:
            obuf[b, own, :] = total
        else:
            gbuf[b, own, :] = total

    def gather_start(b, level):
        axis, me, n, _, _, size, base = axes[level]
        own = rows_at(base + me * size, size)
        copies = []
        for o in range(1, n):
            peer = lax.rem(me + o, n)
            copy = remote(obuf.at[b, own], obuf.at[b, own], {axis: peer})
            copy.start()
            copies.append(copy)
        pending.append(copies)
        return copies

    def arrive(copies):
        for copy in copies:
            copy.wait_recv()

    def small_start(level):
        axis, me, n, _, slots, _, _ = axes[level]
        slots[me] = small[...]
        copies = []
        for o in range(1, n):
            peer = lax.rem(me + o, n)
            copy = remote(slots.at[me], slots.at[me], {axis: peer})
            copy.start()
            copies.append(copy)
        pending.append(copies)
        return copies

    def small_end(level, copies):
        n, slots = axes[level][2], axes[level][4]
        arrive(copies)
        total = slots[0]
        for i in range(1, n):
            total = total + slots[i]
        small[...] = total

    weight_grads(1)
    red2 = scatter_start(1, 0)
    for k in range(TAPS):
        total = jnp.zeros((1, 128), F32)
        for c in range(CHUNKS):
            both = gpad2[c, HALF:HALF + segs] * pad2[c, k:k + segs]
            total = total + jnp.sum(both.reshape(crow, 128), axis=0, keepdims=True)
        small[k:k + 1, :] = total

    gain_sum = jnp.zeros((1, 128), F32)
    for step, c in enumerate(ORDER):
        ghalo2[c].wait()
        at = pl.ds(c * crow, crow)
        gnorm = tap(1, TAPS - 1) * gpad2[c, 0:segs].reshape(crow, 128)
        for k in range(1, TAPS):
            gnorm = gnorm + tap(1, TAPS - 1 - k) * gpad2[c, k:k + segs].reshape(crow, 128)
        s = st1[at]
        r = inv_rms(s)
        xhat = s * r
        gain_sum = gain_sum + jnp.sum(gnorm * xhat, axis=0, keepdims=True)
        q = gnorm * gain2
        g = gather(ct_ref.at[0], c, 0) + r * (q - xhat * jnp.mean(q * xhat, axis=-1, keepdims=True))
        gconv = backward_head(0, c, g)
        for j in range(segs):
            lo = j * D2 + c * RES
            g1[lo:lo + RES, :] = g[j * RES:(j + 1) * RES, :]
            gpad1[rim + lo:rim + lo + RES, :] = gconv[j * RES:(j + 1) * RES, :]
        if step == 1:
            scatter_end(1, 0, red2)
            red2 = scatter_start(1, 1)
    small[7:8, :] = gain_sum
    ghalo1 = rim_halo(gpad1)
    ghalo1.start()
    weight_grads(0)
    red1 = scatter_start(0, 0)
    scatter_end(1, 1, red2)
    red2 = scatter_start(1, 2)
    for k in range(TAPS):
        both = gpad1[rim:rim + rows_total, :] * pad1[k * D1:k * D1 + rows_total, :]
        small[8 + k:9 + k, :] = jnp.sum(both, axis=0, keepdims=True)

    scatter_end(0, 0, red1)
    red1 = scatter_start(0, 1)

    gain_sum = jnp.zeros((1, 128), F32)
    waited = False
    blocks = rows_total // D2
    for q_i in [i for i in range(1, blocks - 1)] + [0, blocks - 1]:
        if q_i in (0, blocks - 1) and not waited:
            ghalo1.wait()
            waited = True
        lo = q_i * D2
        gnorm = tap(0, TAPS - 1) * gpad1[lo:lo + D2, :]
        for k in range(1, TAPS):
            gnorm = gnorm + tap(0, TAPS - 1 - k) * gpad1[lo + k * D1:lo + k * D1 + D2, :]
        s = x_ref[0, lo:lo + D2, :]
        r = inv_rms(s)
        xhat = s * r
        gain_sum = gain_sum + jnp.sum(gnorm * xhat, axis=0, keepdims=True)
        q = gnorm * gain1
        gx_ref[0, lo:lo + D2, :] = g1[lo:lo + D2, :] + r * (
            q - xhat * jnp.mean(q * xhat, axis=-1, keepdims=True)
        )
    small[15:16, :] = gain_sum

    tiny = small_start(0)
    scatter_end(1, 2, red2)
    all2 = gather_start(1, 2)
    scatter_end(0, 1, red1)
    red1 = scatter_start(0, 2)
    small_end(0, tiny)
    tiny = small_start(1)
    arrive(all2)
    all2 = gather_start(1, 1)
    scatter_end(0, 2, red1)
    all1 = gather_start(0, 2)
    small_end(1, tiny)
    tiny = small_start(2)
    arrive(all2)
    all2 = gather_start(1, 0)
    arrive(all1)
    all1 = gather_start(0, 1)
    small_end(2, tiny)
    arrive(all2)

    def write_out(b):
        gwi_ref[b, :, 0:128] = obuf[b, 0:128, :]
        gwi_ref[b, :, 128:256] = obuf[b, 128:256, :]
        gwo_ref[b] = obuf[b, 256:512, :]

    write_out(1)
    gt_ref[1] = small[0:7, :]
    gg_ref[1:2, :] = small[7:8, :]
    gt_ref[0] = small[8:15, :]
    gg_ref[0:1, :] = small[15:16, :]
    arrive(all1)
    all1 = gather_start(0, 0)
    arrive(all1)
    write_out(0)

    for item in pending:
        if isinstance(item, list):
            for copy in item:
                copy.wait_send()
        else:
            item.finish()


def local(nctx, ndp, nrep, features, cotangent, norm_gains, depth_taps, w_in, w_out):
    rows = features.shape[1]
    unit = 8 * nctx * ndp * nrep
    grad_rows = -(-512 // unit) * unit
    half = grad_rows // nrep
    quarter = half // ndp
    piece = quarter // nctx
    rim = HALF * D1
    wide = rows // D2 + 2 * HALF
    sems = 4 + 4 * CHUNKS + 5 * (nctx + ndp + nrep)
    vmem = pltpu.VMEM

    def peers(n):
        return max(n - 1, 1)

    return pl.pallas_call(
        functools.partial(kernel, nctx, ndp, nrep, rows, grad_rows),
        out_shape=(
            jax.ShapeDtypeStruct(features.shape, F32),
            jax.ShapeDtypeStruct(norm_gains.shape, F32),
            jax.ShapeDtypeStruct(depth_taps.shape, F32),
            jax.ShapeDtypeStruct(w_in.shape, F32),
            jax.ShapeDtypeStruct(w_out.shape, F32),
        ),
        in_specs=[pl.BlockSpec(memory_space=vmem)] * 6,
        out_specs=tuple([pl.BlockSpec(memory_space=vmem)] * 5),
        scratch_shapes=[
            vmem((rows + 2 * rim, 128), F32),
            vmem((rows + 2 * rim, 128), F32),
            vmem((CHUNKS, wide, RES, 128), F32),
            vmem((CHUNKS, wide, RES, 128), F32),
            vmem((rows, 128), F32),
            vmem((rows, 128), F32),
            vmem((2, 128, 256), BF16),
            vmem((2, 128, 256), BF16),
            vmem((2, 256, 128), BF16),
            vmem((2, 256, 128), BF16),
            vmem((2, rows, 128), BF16),
            vmem((2, rows, 128), BF16),
            vmem((2, rows, 256), BF16),
            vmem((2, rows, 256), BF16),
            vmem((2, rows, 256), F32),
            vmem((2, rows, 128), BF16),
            vmem((2, rows, 128), BF16),
            vmem((2, rows, 256), BF16),
            vmem((2, rows, 256), BF16),
            vmem((2, grad_rows, 128), F32),
            vmem((2, grad_rows, 128), F32),
            vmem((2, peers(nrep), half, 128), F32),
            vmem((2, peers(ndp), quarter, 128), F32),
            vmem((2, peers(nctx), piece, 128), F32),
            vmem((16, 128), F32),
            vmem((nrep, 16, 128), F32),
            vmem((ndp, 16, 128), F32),
            vmem((nctx, 16, 128), F32),
            pltpu.SemaphoreType.DMA((sems,)),
            pltpu.SemaphoreType.DMA((sems,)),
        ],
        compiler_params=pltpu.CompilerParams(
            collective_id=0, has_side_effects=True, vmem_limit_bytes=40 * 1024 * 1024
        ),
    )(features, cotangent, norm_gains, depth_taps, w_in, w_out)


def solution(mesh):
    sizes = dict(mesh.shape)
    return jax.shard_map(
        functools.partial(local, sizes["ctx"], sizes["dp"], sizes["rep"]),
        mesh=mesh,
        in_specs=(
            P(("groups", "dp", "rep"), "ctx", None),
            P(("groups", "dp", "rep"), "ctx", None),
            P(),
            P(),
            P(),
            P(),
        ),
        out_specs=(
            P(("groups", "dp", "rep"), "ctx", None),
            P("groups", None),
            P("groups", None, None),
            P("groups", None, None),
            P("groups", None, None),
        ),
        check_vma=False,
    )
```

time: 172 us -> 52.5 us (0.31)
  waiting for transfers between devices: 69.3 us -> 0 us
  Pallas kernels: 0 us -> 43.5 us
  blocking collectives: 31.2 us -> 0 us
  starting transfers between devices: 23.6 us -> 0 us
  matrix products: 15.3 us -> 0 us
  between operations: 14.9 us -> 0.65 us
  other arithmetic: 7.23 us -> 0 us
    psum x1 -> x0, waiting for transfers between devices: 55 us -> none  [local(): lax.psum((gain_total, taps_total, input_weight_sum, wout_total), ('ctx',...]
    pallas_call x0 -> x1, Pallas kernels: none -> 43.5 us  [local(): pl.pallas_call(functools.partial(kernel, nctx, ndp, nrep, rows, grad_rows...]
    psum x1 -> x0, blocking collectives: 31.2 us -> none  [local(): lax.psum((gain_total, taps_total, input_weight_sum, wout_total), ('ctx',...]
    ppermute x8 -> x0, starting transfers between devices: 23.5 us -> none  [the longest x4 18.2 us: with_halo(): lax.ppermute(lax.slice_in_dim(block, block.shape[dim] - width, None, axis...]
    dot_general x11 -> x0, matrix products: 15.3 us -> none  [the longest x2 3.78 us: backward_block(): jnp.einsum('brh,brc->hc', act_out, grad_out, precision=lax.Precision.HIGH...]
    ppermute x8 -> x0, waiting for transfers between devices: 14.2 us -> none  [the longest x4 11.7 us: with_halo(): lax.ppermute(lax.slice_in_dim(block, 0, width, axis=dim), axis, backward)]
    reduce_sum x3 -> x0, other arithmetic: 3.39 us -> none  [the longest x2 2.14 us: rms_norm(): return stream * scale * gain_vec]
    add x4 -> x0, other arithmetic: 1.95 us -> none  [the longest x2 1.48 us: backward_block(): return (grad_stream + grad_out, (grad_gain, grad_tapw, grad_win, grad_wout))]
  transfers between devices with their start and end apart: 9 -> 0, of which waited for: 6 -> 0; matrix products, arithmetic and copies ran while one was open for 5% -> 0% of each run, Pallas kernels for 0% -> 0%
where the time goes in v1:
time: 52.5 us; the launch traced here: 52.2 us
  Pallas kernels  43.5 us (83%)
  local copies, waits for them, and re-layouts  8.04 us (15%)
  between operations  0.65 us (1%)
    pallas_call x1, Pallas kernels, local(): pl.pallas_call(functools.partial(kernel, nctx, ndp, nrep, rows, grad_rows...  43.5 us
    unnamed x15, local copies, waits for them, and re-layouts  7.45 us

profile of v1, /device:TPU:0, one launch (start us, length us, event | category | flops | bytes accessed | tf_op | source)
XLA Modules:
  0.0 52.2 jit_solution(8254561612115793694)
XLA Ops:
  0.6 0.0 copy-start.4
  0.6 0.7 %copy.11.taps_ref = f32[2,7,128]{2,1,0:T(8,128)S(1)} copy(f32[2,7,128]{2,0,1:T(2,128)} %param.9) | data formatting | bytes 14336 | tf_op args[3]
  1.3 0.0 copy-done.4
  1.3 0.0 copy-start
  1.3 1.0 %copy-done = f32[1,1024,128]{2,1,0:T(8,128)S(1)} copy-done((f32[1,1024,128]{2,1,0:T(8,128)S(1)}, f32[1,1024,128]{2,1,0:T(8,128)}, u32[]{:S(2)}) %copy-start) | copy-done | bytes 524312
  2.4 0.0 copy-start.1
  2.4 1.0 %copy-done.1 = f32[1,1024,128]{2,1,0:T(8,128)S(1)} copy-done((f32[1,1024,128]{2,1,0:T(8,128)S(1)}, f32[1,1024,128]{2,1,0:T(8,128)}, u32[]{:S(2)}) %copy-start.1) | copy-done | bytes 524312
  3.4 0.0 copy-start.2
  3.4 0.9 %copy-done.2 = f32[2,128,256]{2,1,0:T(8,128)S(1)} copy-done((f32[2,128,256]{2,1,0:T(8,128)S(1)}, f32[2,128,256]{2,1,0:T(8,128)}, u32[]{:S(2)}) %copy-start.2) | copy-done | bytes 262168
  4.4 0.0 copy-start.3
  4.4 0.9 %copy-done.3 = f32[2,256,128]{2,1,0:T(8,128)S(1)} copy-done((f32[2,256,128]{2,1,0:T(8,128)S(1)}, f32[2,256,128]{2,1,0:T(8,128)}, u32[]{:S(2)}) %copy-start.3) | copy-done | bytes 262168
  5.3 43.5 %shard_map.101 = (f32[1,1024,128]{2,1,0:T(8,128)S(1)}, f32[2,128]{1,0:T(2,128)S(1)}, f32[2,7,128]{2,1,0:T(8,128)S(1)}, f32[2,128,256]{2,1,0:T(8,128)S(1)}, f32[2,256,128]{2,1,0:T(8,128)S(1)}) custom-call(f32[1,1024,128]{2,1,0:T(8,128)S(1)} %copy-done, f32[1,1024,128]{2,1,0:T(8,128)S(1)} %copy-done.1, f32[2,128]{1,0:T(2,128)S(1)} %copy-done.4, ...), custom_call_target="tpu_custom_call" | custom-call | tf_op jit(solution)/shard_map/pallas_call | solution.py:425
  48.8 0.6 %copy.12 = f32[2,7,128]{2,0,1:T(2,128)} copy(f32[2,7,128]{2,1,0:T(8,128)S(1)} %get-tuple-element.7) | data formatting | bytes 14336 | tf_op jit(solution)/shard_map/pallas_call | solution.py:425
  49.4 0.8 %copy.17 = f32[1,1024,128]{2,1,0:T(8,128)} copy(f32[1,1024,128]{2,1,0:T(8,128)S(1)} %get-tuple-element.15) | data formatting | bytes 1048576
  50.2 0.6 %copy.18 = f32[2,128]{1,0:T(2,128)} copy(f32[2,128]{1,0:T(2,128)S(1)} %get-tuple-element.16) | data formatting | bytes 2048
  50.8 0.7 %copy.19 = f32[2,128,256]{2,1,0:T(8,128)} copy(f32[2,128,256]{2,1,0:T(8,128)S(1)} %get-tuple-element.18) | data formatting | bytes 524288
  51.5 0.7 %copy.20 = f32[2,256,128]{2,1,0:T(8,128)} copy(f32[2,256,128]{2,1,0:T(8,128)S(1)} %get-tuple-element.19) | data formatting | bytes 524288
Async XLA Ops:
  0.6 0.7 %copy-start.4 = (f32[2,128]{1,0:T(2,128)S(1)}, f32[2,128]{1,0:T(2,128)}, u32[]{:S(2)}) copy-start(f32[2,128]{1,0:T(2,128)} %gain_ref.1) | copy-start | bytes 3076
  1.3 1.0 %copy-start = (f32[1,1024,128]{2,1,0:T(8,128)S(1)}, f32[1,1024,128]{2,1,0:T(8,128)}, u32[]{:S(2)}) copy-start(f32[1,1024,128]{2,1,0:T(8,128)} %x_ref.1) | copy-start | bytes 1572868
  2.4 1.0 %copy-start.1 = (f32[1,1024,128]{2,1,0:T(8,128)S(1)}, f32[1,1024,128]{2,1,0:T(8,128)}, u32[]{:S(2)}) copy-start(f32[1,1024,128]{2,1,0:T(8,128)} %ct_ref.1) | copy-start | bytes 1572868
  3.4 0.9 %copy-start.2 = (f32[2,128,256]{2,1,0:T(8,128)S(1)}, f32[2,128,256]{2,1,0:T(8,128)}, u32[]{:S(2)}) copy-start(f32[2,128,256]{2,1,0:T(8,128)} %win_ref.1) | copy-start | bytes 786436
  4.4 0.9 %copy-start.3 = (f32[2,256,128]{2,1,0:T(8,128)S(1)}, f32[2,256,128]{2,1,0:T(8,128)}, u32[]{:S(2)}) copy-start(f32[2,256,128]{2,1,0:T(8,128)} %wout_ref.1) | copy-start | bytes 786436

commit v2 on v1

--- a/solution.py
+++ b/solution.py
@@ -20,7 +20,6 @@
 ORDER = (1, 2, 0, 3)
 
 NN = (((1,), (0,)), ((), ()))
-NT = (((1,), (1,)), ((), ()))
 TN = (((0,), (0,)), ((), ()))
 
 
@@ -29,11 +28,17 @@
     return high, (v - high.astype(F32)).astype(BF16)
 
 
-def dot3(ah, al, bh, bl, dims):
-    def dot(a, b):
-        return lax.dot_general(a, b, dims, preferred_element_type=F32)
-
-    return dot(ah, bh) + (dot(ah, bl) + dot(al, bh))
+def dot(a, b, dims=NN):
+    return lax.dot_general(a, b, dims, preferred_element_type=F32)
+
+
+def expand(pair, dup, low):
+    return dot(pair, dup) + dot(pair[:, 0:128], low)
+
+
+def contract(high, low, cat):
+    both = dot(high, cat)
+    return both[:, 0:128] + (both[:, 128:256] + dot(low, cat[:, 0:128]))
 
 
 def inv_rms(v):
@@ -48,11 +53,12 @@
 
 def kernel(
     nctx, ndp, nrep, rows_total, grad_rows,
-    x_ref, ct_ref, gain_ref, taps_ref, win_ref, wout_ref,
+    x_hbm, ct_hbm, gain_hbm, taps_hbm, win_hbm, wout_hbm,
     gx_ref, gg_ref, gt_ref, gwi_ref, gwo_ref,
+    x_ref, ct_ref, gain_ref, taps_ref, win_ref, wout_ref, load_sem,
     pad1, gpad1, pad2, gpad2, st1, g1,
-    wih, wil, woh, wol,
-    ch, cl, ah, al, dact, gh, gl, ph, plo,
+    in_dup, in_low, out_cat, outt_dup, outt_low, int_cat,
+    chl, ah, al, dact, ghl, ph, plo,
     gbuf, obuf, rec_a, rec_b, rec_c, small, sm_a, sm_b, sm_c,
     send_sem, recv_sem,
 ):
@@ -77,15 +83,38 @@
             device_id=device, device_id_type=MESH,
         )
 
+    loads = [
+        pltpu.make_async_copy(src, dst, load_sem.at[i])
+        for i, (src, dst) in enumerate(
+            (
+                (gain_hbm, gain_ref), (x_hbm, x_ref), (taps_hbm, taps_ref),
+                (win_hbm, win_ref), (wout_hbm, wout_ref), (ct_hbm, ct_ref),
+            )
+        )
+    ]
+    for load in loads:
+        load.start()
+
     barrier = pltpu.get_barrier_semaphore()
+    def on_rep(p):
+        return {"rep": p}
+
+    def on_dp(p):
+        return {"dp": p}
+
+    def on_ctx(p):
+        return {"ctx": p}
+
     greeted = 0
-    for axis, me, n in (("ctx", zi, nctx), ("dp", di, ndp), ("rep", ri, nrep)):
+    for place, me, n in ((on_ctx, zi, nctx), (on_dp, di, ndp), (on_rep, ri, nrep)):
         for o in range(1, n):
             pl.semaphore_signal(
-                barrier, inc=1, device_id={axis: lax.rem(me + o, n)}, device_id_type=MESH
+                barrier, inc=1, device_id=place(lax.rem(me + o, n)), device_id_type=MESH
             )
             greeted += 1
 
+    loads[0].wait()
+    loads[1].wait()
     gain1 = gain_ref[0:1, :]
     gain2 = gain_ref[1:2, :]
 
@@ -95,6 +124,19 @@
 
     norm_rows(0, rim)
     norm_rows(rows_total - rim, rim)
+    for load in loads[2:5]:
+        load.wait()
+    for b in range(2):
+        high, low = split(win_ref[b])
+        in_dup[b] = jnp.concatenate([high, high], axis=0)
+        in_low[b] = low
+        high, low = split(win_ref[b].T)
+        int_cat[b] = jnp.concatenate([high, low], axis=1)
+        high, low = split(wout_ref[b])
+        out_cat[b] = jnp.concatenate([high, low], axis=1)
+        high, low = split(wout_ref[b].T)
+        outt_dup[b] = jnp.concatenate([high, high], axis=0)
+        outt_low[b] = low
     pl.semaphore_wait(barrier, greeted)
 
     class Halo:
@@ -161,10 +203,6 @@
         gpad2[:, HALF + segs:] = jnp.zeros((CHUNKS, HALF, RES, 128), F32)
 
     norm_rows(rim, rows_total - 2 * rim)
-    for b in range(2):
-        wih[b], wil[b] = split(win_ref[b])
-        woh[b], wol[b] = split(wout_ref[b])
-
     def gather(ref, c, base):
         return jnp.concatenate(
             [ref[base + j * D2 + c * RES:base + j * D2 + (c + 1) * RES, :] for j in range(segs)],
@@ -172,32 +210,32 @@
         )
 
     def tap(b, k):
-        return taps_ref[b, k:k + 1, :]
+        return taps_ref[k, b:b + 1, :]
 
     def forward_tail(b, c, conv):
         at = pl.ds(c * crow, crow)
-        cth, ctl = split(conv)
-        ch[b, at], cl[b, at] = cth, ctl
-        pre = dot3(cth, ctl, wih[b], wil[b], NN)
-        act, slope = silu_pair(pre)
+        pair = jnp.concatenate(split(conv), axis=1)
+        chl[b, at] = pair
+        act, slope = silu_pair(expand(pair, in_dup[b], in_low[b]))
         dact[b, at] = slope
-        ath, atl = split(act)
-        ah[b, at], al[b, at] = ath, atl
+        ah[b, at], al[b, at] = split(act)
 
     def backward_head(b, c, g):
         at = pl.ds(c * crow, crow)
-        gth, gtl = split(g)
-        gh[b, at], gl[b, at] = gth, gtl
-        gpre = dot3(gth, gtl, woh[b], wol[b], NT) * dact[b, at]
-        pth, ptl = split(gpre)
-        ph[b, at], plo[b, at] = pth, ptl
-        return dot3(pth, ptl, wih[b], wil[b], NT)
+        pair = jnp.concatenate(split(g), axis=1)
+        ghl[b, at] = pair
+        high, low = split(expand(pair, outt_dup[b], outt_low[b]) * dact[b, at])
+        ph[b, at], plo[b, at] = high, low
+        return contract(high, low, int_cat[b])
 
     def weight_grads(b):
-        gwi = dot3(ch[b], cl[b], ph[b], plo[b], TN)
+        both = dot(chl[b], ph[b], TN)
+        gwi = both[0:128] + (both[128:256] + dot(chl[b, :, 0:128], plo[b], TN))
         gbuf[b, 0:128, :] = gwi[:, 0:128]
         gbuf[b, 128:256, :] = gwi[:, 128:256]
-        gbuf[b, 256:512, :] = dot3(ah[b], al[b], gh[b], gl[b], TN)
+        both = dot(ghl[b], ah[b], TN)
+        gwo = both[0:128] + (both[128:256] + dot(ghl[b, :, 0:128], al[b], TN))
+        gbuf[b, 256:512, :] = gwo.T
 
     halo2 = [seg_halo(pad2, c) for c in range(CHUNKS)]
     waited = False
@@ -210,10 +248,12 @@
             conv = conv + tap(0, k) * gather(pad1, c, k * D1)
         forward_tail(0, c, conv)
         at = pl.ds(c * crow, crow)
-        s = gather(x_ref.at[0], c, 0) + dot3(ah[0, at], al[0, at], woh[0], wol[0], NN)
+        s = gather(x_ref.at[0], c, 0) + contract(ah[0, at], al[0, at], out_cat[0])
         st1[at] = s
         pad2[c, HALF:HALF + segs] = (s * inv_rms(s) * gain2).reshape(segs, RES, 128)
         halo2[c].start()
+
+    loads[5].wait()
 
     ghalo2 = [seg_halo(gpad2, c) for c in range(CHUNKS)]
     for c in ORDER:
@@ -230,21 +270,21 @@
     quarter = half // ndp
     piece = quarter // nctx
     axes = (
-        ("rep", ri, nrep, rec_a, sm_a, half, 0),
-        ("dp", di, ndp, rec_b, sm_b, quarter, ri * half),
-        ("ctx", zi, nctx, rec_c, sm_c, piece, ri * half + di * quarter),
+        (on_rep, ri, nrep, rec_a, sm_a, half, 0),
+        (on_dp, di, ndp, rec_b, sm_b, quarter, ri * half),
+        (on_ctx, zi, nctx, rec_c, sm_c, piece, ri * half + di * quarter),
     )
 
     def rows_at(start, size):
         return pl.ds(pl.multiple_of(start, 8), size)
 
     def scatter_start(b, level):
-        axis, me, n, rec, _, size, base = axes[level]
+        place, me, n, rec, _, size, base = axes[level]
         copies = []
         for o in range(1, n):
             peer = lax.rem(me + o, n)
             copy = remote(
-                gbuf.at[b, rows_at(base + peer * size, size)], rec.at[b, o - 1], {axis: peer}
+                gbuf.at[b, rows_at(base + peer * size, size)], rec.at[b, o - 1], place(peer)
             )
             copy.start()
             copies.append(copy)
@@ -252,7 +292,7 @@
         return copies
 
     def scatter_end(b, level, copies):
-        axis, me, n, rec, _, size, base = axes[level]
+        place, me, n, rec, _, size, base = axes[level]
         own = rows_at(base + me * size, size)
         total = gbuf[b, own, :]
         for o in range(1, n):
@@ -264,12 +304,12 @@
             gbuf[b, own, :] = total
 
     def gather_start(b, level):
-        axis, me, n, _, _, size, base = axes[level]
+        place, me, n, _, _, size, base = axes[level]
         own = rows_at(base + me * size, size)
         copies = []
         for o in range(1, n):
             peer = lax.rem(me + o, n)
-            copy = remote(obuf.at[b, own], obuf.at[b, own], {axis: peer})
+            copy = remote(obuf.at[b, own], obuf.at[b, own], place(peer))
             copy.start()
             copies.append(copy)
         pending.append(copies)
@@ -280,12 +320,12 @@
             copy.wait_recv()
 
     def small_start(level):
-        axis, me, n, _, slots, _, _ = axes[level]
+        place, me, n, _, slots, _, _ = axes[level]
         slots[me] = small[...]
         copies = []
         for o in range(1, n):
             peer = lax.rem(me + o, n)
-            copy = remote(slots.at[me], slots.at[me], {axis: peer})
+            copy = remote(slots.at[me], slots.at[me], place(peer))
             copy.start()
             copies.append(copy)
         pending.append(copies)
@@ -364,6 +404,11 @@
         )
     small[15:16, :] = gain_sum
 
+    def write_out(b):
+        gwi_ref[b, :, 0:128] = obuf[b, 0:128, :]
+        gwi_ref[b, :, 128:256] = obuf[b, 128:256, :]
+        gwo_ref[b] = obuf[b, 256:512, :]
+
     tiny = small_start(0)
     scatter_end(1, 2, red2)
     all2 = gather_start(1, 2)
@@ -383,19 +428,14 @@
     all1 = gather_start(0, 1)
     small_end(2, tiny)
     arrive(all2)
-
-    def write_out(b):
-        gwi_ref[b, :, 0:128] = obuf[b, 0:128, :]
-        gwi_ref[b, :, 128:256] = obuf[b, 128:256, :]
-        gwo_ref[b] = obuf[b, 256:512, :]
-
     write_out(1)
-    gt_ref[1] = small[0:7, :]
-    gg_ref[1:2, :] = small[7:8, :]
-    gt_ref[0] = small[8:15, :]
-    gg_ref[0:1, :] = small[15:16, :]
     arrive(all1)
     all1 = gather_start(0, 0)
+    for k in range(TAPS):
+        gt_ref[k, 0:1, :] = small[8 + k:9 + k, :]
+        gt_ref[k, 1:2, :] = small[k:k + 1, :]
+    gg_ref[1:2, :] = small[7:8, :]
+    gg_ref[0:1, :] = small[15:16, :]
     arrive(all1)
     write_out(0)
 
@@ -405,6 +445,15 @@
                 copy.wait_send()
         else:
             item.finish()
+
+
+def publish(*refs):
+    srcs, dsts, sem = refs[:5], refs[5:10], refs[10]
+    copies = [pltpu.make_async_copy(srcs[i], dsts[i], sem.at[i]) for i in range(5)]
+    for copy in copies:
+        copy.start()
+    for copy in copies:
+        copy.wait()
 
 
 def local(nctx, ndp, nrep, features, cotangent, norm_gains, depth_taps, w_in, w_out):
@@ -422,35 +471,38 @@
     def peers(n):
         return max(n - 1, 1)
 
-    return pl.pallas_call(
+    taps = jnp.transpose(depth_taps, (1, 0, 2))
+    args = tuple(
+        pltpu.with_memory_space_constraint(a, pltpu.HBM)
+        for a in (features, cotangent, norm_gains, taps, w_in, w_out)
+    )
+    shapes = tuple(
+        jax.ShapeDtypeStruct(a.shape, F32) for a in (features, norm_gains, taps, w_in, w_out)
+    )
+    results = pl.pallas_call(
         functools.partial(kernel, nctx, ndp, nrep, rows, grad_rows),
-        out_shape=(
-            jax.ShapeDtypeStruct(features.shape, F32),
-            jax.ShapeDtypeStruct(norm_gains.shape, F32),
-            jax.ShapeDtypeStruct(depth_taps.shape, F32),
-            jax.ShapeDtypeStruct(w_in.shape, F32),
-            jax.ShapeDtypeStruct(w_out.shape, F32),
-        ),
-        in_specs=[pl.BlockSpec(memory_space=vmem)] * 6,
+        out_shape=shapes,
+        in_specs=[pl.BlockSpec(memory_space=pltpu.HBM)] * 6,
         out_specs=tuple([pl.BlockSpec(memory_space=vmem)] * 5),
-        scratch_shapes=[
+        scratch_shapes=[vmem(a.shape, F32) for a in args] + [
+            pltpu.SemaphoreType.DMA((6,)),
             vmem((rows + 2 * rim, 128), F32),
             vmem((rows + 2 * rim, 128), F32),
             vmem((CHUNKS, wide, RES, 128), F32),
             vmem((CHUNKS, wide, RES, 128), F32),
             vmem((rows, 128), F32),
             vmem((rows, 128), F32),
+            vmem((2, 256, 256), BF16),
             vmem((2, 128, 256), BF16),
+            vmem((2, 256, 256), BF16),
+            vmem((2, 256, 256), BF16),
             vmem((2, 128, 256), BF16),
-            vmem((2, 256, 128), BF16),
-            vmem((2, 256, 128), BF16),
-            vmem((2, rows, 128), BF16),
-            vmem((2, rows, 128), BF16),
+            vmem((2, 256, 256), BF16),
+            vmem((2, rows, 256), BF16),
             vmem((2, rows, 256), BF16),
             vmem((2, rows, 256), BF16),
             vmem((2, rows, 256), F32),
-            vmem((2, rows, 128), BF16),
-            vmem((2, rows, 128), BF16),
+            vmem((2, rows, 256), BF16),
             vmem((2, rows, 256), BF16),
             vmem((2, rows, 256), BF16),
             vmem((2, grad_rows, 128), F32),
@@ -468,7 +520,16 @@
         compiler_params=pltpu.CompilerParams(
             collective_id=0, has_side_effects=True, vmem_limit_bytes=40 * 1024 * 1024
         ),
-    )(features, cotangent, norm_gains, depth_taps, w_in, w_out)
+    )(*args)
+    gx, gg, gt, gwi, gwo = pl.pallas_call(
+        publish,
+        out_shape=shapes,
+        in_specs=[pl.BlockSpec(memory_space=pl.ANY)] * 5,
+        out_specs=tuple([pl.BlockSpec(memory_space=pltpu.HBM)] * 5),
+        compiler_params=pltpu.CompilerParams(vmem_limit_bytes=4 * 1024 * 1024),
+        scratch_shapes=[pltpu.SemaphoreType.DMA((5,))],
+    )(*results)
+    return gx, gg, jnp.transpose(gt, (1, 0, 2)), gwi, gwo
 
 
 def solution(mesh):

time: 52.5 us -> 45.1 us (0.86)
  local copies, waits for them, and re-layouts: 8.04 us -> 0 us
  Pallas kernels: 43.5 us -> 44.3 us
    unnamed x15 -> x0, local copies, waits for them, and re-layouts: 7.45 us -> none
    pallas_call x0 -> x1, Pallas kernels: none -> 1.02 us  [local(): pl.pallas_call(publish, out_shape=shapes, in_specs=[pl.BlockSpec(memory_s...]
    pallas_call x1 -> x0, local copies, waits for them, and re-layouts: 0.6 us -> none  [local(): pl.pallas_call(functools.partial(kernel, nctx, ndp, nrep, rows, grad_rows...]
where the time goes in v2:
time: 45.1 us; the launch traced here: 45 us
  Pallas kernels  44.3 us (98%)
  between operations  0.64 us (1%)
    pallas_call x1, Pallas kernels, local(): pl.pallas_call(functools.partial(kernel, nctx, ndp, nrep, rows, grad_rows...  43.3 us
    pallas_call x1, Pallas kernels, local(): pl.pallas_call(publish, out_shape=shapes, in_specs=[pl.BlockSpec(memory_s...  1.02 us

profile of v2, /device:TPU:0, one launch (start us, length us, event | category | flops | bytes accessed | tf_op | source)
XLA Modules:
  0.0 45.0 jit_solution(17192738879820950765)
XLA Ops:
  0.6 43.3 %shard_map.101 = (f32[1,1024,128]{2,1,0:T(8,128)S(1)}, f32[2,128]{1,0:T(2,128)S(1)}, f32[7,2,128]{2,1,0:T(2,128)S(1)}, f32[2,128,256]{2,1,0:T(8,128)S(1)}, f32[2,256,128]{2,1,0:T(8,128)S(1)}) custom-call(f32[1,1024,128]{2,1,0:T(8,128)} %x_hbm.1, f32[1,1024,128]{2,1,0:T(8,128)} %ct_hbm.1, f32[2,128]{1,0:T(2,128)} %gain_hbm.1, f32[7,2,128]{2,1,0:T(2,128)} %bitcast.2, ...), custom_call_target="tpu_custom_call" | custom-call | tf_op jit(solution)/shard_map/pallas_call | solution.py:482
  43.9 1.0 %shard_map.102 = (f32[1,1024,128]{2,1,0:T(8,128)}, f32[2,128]{1,0:T(2,128)}, f32[7,2,128]{2,1,0:T(2,128)}, f32[2,128,256]{2,1,0:T(8,128)}, f32[2,256,128]{2,1,0:T(8,128)}) custom-call(f32[1,1024,128]{2,1,0:T(8,128)S(1)} %get-tuple-element.15.refs_0_, f32[2,128]{1,0:T(2,128)S(1)} %get-tuple-element.16.refs_1_, f32[7,2,128]{2,1,0:T(2,128)S(1)} %get-tuple-element.17.refs_2_, ...), custom_call_target="tpu_custom_call" | custom-call | tf_op jit(solution)/shard_map/pallas_call | solution.py:524
